TPU v7x, 512 devices: a whole 4x8x8 slice. The times are simulated.
512 devices in a mesh: dp: 32 (over z, x), expert: 16 (over y, core).
Axes of the slice: x: 4, y: 8, z: 8, core: 2. Of those that a mesh axis runs over, the one named last changes fastest.
Arguments:
- tokens: bfloat16 [100352, 1024], P(('dp', 'expert')), may hold values from -6 to 6
- route_weight: bfloat16 [100352], P(('dp', 'expert')), may hold values from 0.29882812 to 1
- expert_ids: int32 [100352, 1], P(('dp', 'expert')), may hold values from 0 to 15; in each aligned block of 196 rows (0 to 195, 196 to 391, ...) at most 24 rows name the same one
- visible: int32 [2048, 49], P(('dp', 'expert')), may hold values from 0 to 195, as said below
- owner_map: int32 [2048], P(('dp', 'expert')), may hold values from 0 to 15, as said below
- norm_gain: float32 [1024], replicated, may hold values from 0.5 to 1.5
- expert_in: bfloat16 [16, 2048, 1024], P('expert', 'dp'), may hold values from -0.1875 to 0.1875
- expert_out: bfloat16 [16, 2048, 1024], P('expert', 'dp'), may hold values from -0.125 to 0.125
- final_gain: float32 [1024], replicated, may hold values from 0.5 to 1.5
- embed_weight: bfloat16 [1024, 512], replicated, may hold values from -0.1875 to 0.1875
- mask_token: bfloat16 [512], replicated, may hold values from -4 to 4
- decoder_pos: bfloat16 [196, 512], replicated, may hold values from -3 to 3
- decoder_gain: float32 [512], replicated, may hold values from 0.5 to 1.5
- attention_in: bfloat16 [512, 1536], replicated
- attention_out: bfloat16 [512, 512], replicated, may hold values from -0.25 to 0.25
Outputs:
- decoded_grid: bfloat16 [2048, 196, 512], P(('dp', 'expert'))
Inputs may be any that keep to these rules, and one draw needn't show every extreme that they name: `expert_ids`: in each aligned block of 196 rows (the tokens of one device) no expert is named by more than 24 rows. `visible`: each row names 49 different positions. `owner_map`: the 4 images of an aligned block (one device) share one owner; in each aligned block of 64 images the 16 blocks have different owners.
All inputs are finite; a program needn't handle non-finite values.
Results may differ from a plain program's by a relative error of at most 0.009.
Values may be sent and summed in bfloat16 or wider, within the bound.
A program may use at most 64 MiB of HBM per device.

v0:
```python
import jax
import jax.numpy as jnp
from jax import lax
from jax.sharding import PartitionSpec as P

D = 1024
HEADS = 16
HEAD_DIM = 32
DD = 512
GRID = 196
VIS = 49
EPSILON = 1e-06


def layer_norm(values, factor):
    values = values.astype(jnp.float32)
    centered = values - jnp.mean(values, axis=-1, keepdims=True)
    variance = jnp.mean(centered * centered, axis=-1, keepdims=True)
    return centered * lax.rsqrt(variance + EPSILON) * factor


def slot_table(token_expert, experts, capacity):
    onehot = (token_expert[:, None] == jnp.arange(experts, dtype=jnp.int32)[None, :]).astype(
        jnp.int32
    )
    earlier = jnp.sum((jnp.cumsum(onehot, axis=0) - onehot) * onehot, axis=1)
    slot_index = token_expert * capacity + earlier
    return (slot_index[:, None] == jnp.arange(experts * capacity, dtype=jnp.int32)[None, :]).astype(
        jnp.bfloat16
    )


def embed_rows(merged, final_gain, embed_weight):
    final_normed = layer_norm(merged, final_gain).astype(jnp.bfloat16)
    return jnp.dot(final_normed, embed_weight, preferred_element_type=jnp.float32).astype(
        jnp.bfloat16
    )


def per_device(
    tokens,
    route_weight,
    expert_ids,
    visible,
    owner_map,
    norm_gain,
    expert_in,
    expert_out,
    final_gain,
    embed_weight,
    mask_token,
    decoder_pos,
    decoder_gain,
    attention_in,
    attention_out,
):
    groups = lax.axis_size("expert")
    tok_dev = tokens.shape[0]
    img_dev = visible.shape[0]
    exp_dev = expert_in.shape[0]
    experts = exp_dev * groups
    capacity = 2 * tok_dev // experts
    own_index = lax.axis_index("expert")
    token_expert = expert_ids[:, 0]
    all_ids, all_visible, all_owner = (
        lax.all_gather(token_expert, "expert", axis=0, tiled=True),
        lax.all_gather(visible, "expert", axis=0, tiled=True),
        lax.all_gather(owner_map, "expert", axis=0, tiled=True),
    )
    placing = slot_table(token_expert, experts, capacity)
    send_rows = jnp.dot(placing.T, tokens, preferred_element_type=jnp.float32).astype(jnp.bfloat16)
    send_weight = jnp.einsum(
        "ts,t->s", placing, route_weight, preferred_element_type=jnp.float32
    ).astype(jnp.bfloat16)
    arrived_rows, arrived_weight = (
        lax.all_to_all(
            send_rows.reshape(groups, exp_dev * capacity, D),
            "expert",
            split_axis=0,
            concat_axis=0,
            tiled=True,
        ),
        lax.all_to_all(
            send_weight.reshape(groups, exp_dev * capacity),
            "expert",
            split_axis=0,
            concat_axis=0,
            tiled=True,
        ),
    )
    expert_rows = (
        arrived_rows.reshape(groups, exp_dev, capacity, D)
        .transpose(1, 0, 2, 3)
        .reshape(exp_dev, groups * capacity, D)
    )
    expert_weight = (
        arrived_weight.reshape(groups, exp_dev, capacity)
        .transpose(1, 0, 2)
        .reshape(exp_dev, groups * capacity)
    )
    normed = layer_norm(expert_rows, norm_gain).astype(jnp.bfloat16)
    piece_in = lax.all_gather(expert_in, "dp", axis=1, tiled=True)
    piece_out = lax.all_gather(expert_out, "dp", axis=1, tiled=True)
    hidden = jax.nn.gelu(
        jnp.einsum("esd,efd->esf", normed, piece_in, preferred_element_type=jnp.float32)
    ).astype(jnp.bfloat16)
    update = jnp.einsum("esf,efd->esd", hidden, piece_out, preferred_element_type=jnp.float32)
    merged = (
        expert_rows.astype(jnp.float32) + expert_weight.astype(jnp.float32)[:, :, None] * update
    ).astype(jnp.bfloat16)
    source_owner = all_owner.reshape(groups, img_dev)[:, 0]
    to_owner = (source_owner[None, :] == jnp.arange(groups, dtype=jnp.int32)[:, None]).astype(
        jnp.bfloat16
    )
    source = jnp.sum(
        jnp.arange(groups, dtype=jnp.int32) * (source_owner == own_index).astype(jnp.int32)
    )
    source_ids = lax.dynamic_slice_in_dim(all_ids, source * tok_dev, tok_dev)
    source_visible = lax.dynamic_slice_in_dim(all_visible, source * img_dev, img_dev)
    source_table = slot_table(source_ids, experts, capacity)
    payload = (
        merged.reshape(exp_dev, groups, capacity, D)
        .transpose(1, 0, 2, 3)
        .reshape(groups, exp_dev * capacity, D)
    )
    outgoing = jnp.einsum(
        "os,scw->ocw", to_owner, payload, preferred_element_type=jnp.float32
    ).astype(jnp.bfloat16)
    arrived = lax.all_to_all(outgoing, "expert", split_axis=0, concat_axis=0, tiled=True)
    own_rows = jnp.dot(
        source_table, arrived.reshape(experts * capacity, D), preferred_element_type=jnp.float32
    ).astype(jnp.bfloat16)
    embedded = embed_rows(own_rows, final_gain, embed_weight)
    image_rows = embedded.reshape(img_dev, 1, VIS, DD)
    image_places = source_visible.reshape(img_dev, 1, VIS)

    def decode_image(operands):
        rows_one, places_one = operands
        position_hit = places_one[:, :, None] == jnp.arange(GRID, dtype=jnp.int32)[None, None, :]
        covered = jnp.any(position_hit, axis=1)
        placed = jnp.einsum(
            "ivg,ivd->igd",
            position_hit.astype(jnp.bfloat16),
            rows_one,
            preferred_element_type=jnp.float32,
        )
        canvas = jnp.where(
            covered[:, :, None], placed, mask_token.astype(jnp.float32)[None, None, :]
        )
        initial = canvas + decoder_pos.astype(jnp.float32)[None]
        dec_normed = layer_norm(initial, decoder_gain).astype(jnp.bfloat16)
        projected = jnp.dot(
            dec_normed.reshape(GRID, DD), attention_in, preferred_element_type=jnp.float32
        ).astype(jnp.bfloat16)
        projected = projected.reshape(1, GRID, 3, HEADS, HEAD_DIM)
        queries = projected[:, :, 0]
        key_rows = projected[:, :, 1]
        value_rows = projected[:, :, 2]
        scores = jnp.einsum(
            "iqhc,ikhc->ihqk", queries, key_rows, preferred_element_type=jnp.float32
        ) * HEAD_DIM ** (-0.5)
        highest = jnp.max(scores, axis=-1, keepdims=True)
        raised = jnp.exp(scores - highest)
        weights = (raised / jnp.sum(raised, axis=-1, keepdims=True)).astype(jnp.bfloat16)
        mixed = jnp.einsum(
            "ihqk,ikhc->iqhc", weights, value_rows, preferred_element_type=jnp.float32
        ).astype(jnp.bfloat16)
        update_out = jnp.dot(
            mixed.reshape(GRID, DD), attention_out, preferred_element_type=jnp.float32
        )
        return (initial + update_out.reshape(1, GRID, DD)).astype(jnp.bfloat16)

    decoded = lax.map(decode_image, (image_rows, image_places))
    return decoded.reshape(img_dev, GRID, DD)


def solution(mesh):
    return jax.shard_map(
        per_device,
        mesh=mesh,
        in_specs=(
            P(("dp", "expert"), None),
            P(("dp", "expert")),
            P(("dp", "expert"), None),
            P(("dp", "expert"), None),
            P(("dp", "expert")),
            P(),
            P("expert", "dp", None),
            P("expert", "dp", None),
            P(),
            P(),
            P(),
            P(),
            P(),
            P(),
            P(),
        ),
        out_specs=P(("dp", "expert"), None, None),
        check_vma=False,
    )
```

profile of v0, /device:TPU:1, one launch (start us, length us, event | category | flops | bytes accessed | tf_op | source)
XLA Modules:
  0.0 293.3 jit_solution(7976622157471527330)
XLA Ops:
  12.6 10.1 %all-to-all-start.1 = ((bf16[16,1,24]{2,1,0:T(2,128)(2,1)}), bf16[16,1,24]{2,1,0:T(2,128)(2,1)S(1)}, u32[]{:S(2)}, u32[]{:S(2)}) async-start(bf16[16,1,24]{2,1,0:T(2,128)(2,1)} %all_to_all.16), calls=%async_computation.1 | async-start | bytes 16384 | tf_op jit(solution)/shard_map/all_to_all | solution.py:83
  22.6 2.4 convolution_convert_fusion.2
  25.0 4.7 %all-to-all-done.1 = bf16[16,1,24]{2,1,0:T(2,128)(2,1)S(1)} async-done(((bf16[16,1,24]{2,1,0:T(2,128)(2,1)}), bf16[16,1,24]{2,1,0:T(2,128)(2,1)S(1)}, u32[]{:S(2)}, u32[]{:S(2)}) %all-to-all-start.1) | async-done | bytes 800 | tf_op jit(solution)/shard_map/all_to_all | solution.py:83
  29.7 4.2 %all-to-all-start = ((bf16[16,24,1024]{2,1,0:T(8,128)(2,1)}), bf16[16,24,1024]{2,1,0:T(8,128)(2,1)S(1)}, u32[]{:S(2)}, u32[]{:S(2)}) async-start(bf16[16,24,1024]{2,1,0:T(8,128)(2,1)} %bitcast.22), calls=%async_computation | async-start | bytes 1572864 | tf_op jit(solution)/shard_map/all_to_all | solution.py:76
  33.9 1.3 dynamic-slice.1
  36.9 55.7 %all-reduce.4 = (s32[64]{0:T(128)S(1)}, s32[3136]{0:T(1024)S(1)}) all-reduce(s32[64]{0:T(128)S(1)} %dynamic-update-slice, s32[3136]{0:T(1024)S(1)} %dynamic-update-slice.1), channel_id=1, replica_groups=mesh['dp'=32,'expert'=16] {'expert'}, use_global_device_ids=true, to_apply=%add.2 | all-reduce | flops 3200 | bytes 25600
  94.1 7.1 %all-gather.5.cloned.1.call-done = bf16[1,2048,1024]{2,1,0:T(8,128)(2,1)} async-done(((bf16[1,64,1024]{2,1,0:T(8,128)(2,1)}), bf16[1,2048,1024]{2,1,0:T(8,128)(2,1)}) %all-gather.5.cloned.1.call-update) | async-done | bytes 4194320 | tf_op jit(solution)/shard_map/all_gather | solution.py:102
  101.2 88.0 %all-gather.7.cloned.1.call-done = bf16[1,2048,1024]{2,1,0:T(8,128)(2,1)} async-done(((bf16[1,64,1024]{2,1,0:T(8,128)(2,1)}), bf16[1,2048,1024]{2,1,0:T(8,128)(2,1)}) %all-gather.7.cloned.1.call-update) | async-done | bytes 4194320 | tf_op jit(solution)/shard_map/all_gather | solution.py:103
  189.2 7.1 %fusion.42 = bf16[384,1024]{1,0:T(8,128)(2,1)S(1)} fusion(bf16[1,2048,1024]{2,1,0:T(8,128)(2,1)} %all-gather.7.cloned.1.call-done, bf16[384,1024]{1,0:T(8,128)(2,1)S(1)} %bitcast.150, bf16[1,2048,1024]{2,1,0:T(8,128)(2,1)} %all-gather.5.cloned.1.call-done, bf16[16,24,1024]{2,1,0:T(8,128)(2,1)S(1)} %all-to-all-done, f32[384]{0:T(512)S(1)} %reshape.421), kind=kOutput, calls=%fused_computation.55 | convolution fusion | flops 3229876224 | bytes 10749440 | tf_op jit(solution)/shard_map/esf,efd->esd/dot_general | solution.py:107
  197.0 1.3 copy.52
  198.3 10.9 %all-to-all-start.2 = ((bf16[16,24,1024]{2,1,0:T(8,128)(2,1)}), bf16[16,24,1024]{2,1,0:T(8,128)(2,1)S(1)}, u32[]{:S(2)}, u32[]{:S(2)}) async-start(bf16[16,24,1024]{2,1,0:T(8,128)(2,1)} %copy.52), calls=%async_computation.2 | async-start | bytes 1572864 | tf_op jit(solution)/shard_map/all_to_all | solution.py:129
  212.3 28.1 %all-gather.1 = s32[16,4,49]{2,1,0:T(4,128)S(1)} all-gather(s32[1,4,49]{2,1,0:T(4,128)S(1)} %bitcast.159), channel_id=1, replica_groups=mesh['dp'=32,'expert'=16] {'expert'}, dimensions={0}, use_global_device_ids=true | all-gather | bytes 13328 | tf_op jit(solution)/shard_map/all_gather | solution.py:67
  242.6 41.3 %while.10 = (s32[]{:T(128)}, bf16[4,1,196,512]{3,2,1,0:T(8,128)(2,1)}, s32[4,1,49]{2,1,0:T(1,128)S(1)}, bf16[4,1,49,512]{3,2,1,0:T(8,128)(2,1)}, bf16[512]{0:T(5...) while((s32[]{:T(128)}, ...), condition=%wide.region_17.18_spmd, body=%wide.region_11.17_spmd.sunk | while | flops 504361024 | bytes 12126609 | solution.py:173
  242.8 1.4 fusion.92
  244.4 1.9 convolution_convert_fusion.6
  246.6 3.0 %fusion.93 = (f32[16,196]{1,0:T(8,128)S(1)}, f32[16,196,196]{1,2,0:T(8,128)}) fusion(bf16[1,196,3,16,32]{1,4,3,2,0:T(8,128)(2,1)S(1)} %bitcast.145), kind=kOutput, calls=%fused_computation.115.clone.1 | convolution fusion | flops 41182148 | bytes 2995456 | tf_op jit(solution)/shard_map/while/body/eval_jaxpr/sub | solution.py:163
  249.6 2.4 fusion.94
  253.1 1.4 fusion.92
  254.7 1.9 convolution_convert_fusion.6
  256.9 3.0 %fusion.93 = (f32[16,196]{1,0:T(8,128)S(1)}, f32[16,196,196]{1,2,0:T(8,128)}) fusion(bf16[1,196,3,16,32]{1,4,3,2,0:T(8,128)(2,1)S(1)} %bitcast.145), kind=kOutput, calls=%fused_computation.115.clone.1 | convolution fusion | flops 41182148 | bytes 2995456 | tf_op jit(solution)/shard_map/while/body/eval_jaxpr/sub | solution.py:163
  259.9 2.4 fusion.94
  262.3 1.0 fusion.95
  263.4 1.4 fusion.92
  265.0 1.9 convolution_convert_fusion.6
  267.3 3.0 %fusion.93 = (f32[16,196]{1,0:T(8,128)S(1)}, f32[16,196,196]{1,2,0:T(8,128)}) fusion(bf16[1,196,3,16,32]{1,4,3,2,0:T(8,128)(2,1)S(1)} %bitcast.145), kind=kOutput, calls=%fused_computation.115.clone.1 | convolution fusion | flops 41182148 | bytes 2995456 | tf_op jit(solution)/shard_map/while/body/eval_jaxpr/sub | solution.py:163
  270.3 2.4 fusion.94
  273.8 1.4 fusion.92
  275.4 1.9 convolution_convert_fusion.6
  277.6 3.0 %fusion.93 = (f32[16,196]{1,0:T(8,128)S(1)}, f32[16,196,196]{1,2,0:T(8,128)}) fusion(bf16[1,196,3,16,32]{1,4,3,2,0:T(8,128)(2,1)S(1)} %bitcast.145), kind=kOutput, calls=%fused_computation.115.clone.1 | convolution fusion | flops 41182148 | bytes 2995456 | tf_op jit(solution)/shard_map/while/body/eval_jaxpr/sub | solution.py:163
  280.6 2.4 fusion.94
  283.0 1.0 fusion.95
  284.0 2.4 copy.67
  (102 shorter events, 16.8 us)
Async XLA Ops:
  6.5 234.9 %copy-start = (bf16[1024,512]{1,0:T(8,128)(2,1)S(1)}, bf16[1024,512]{1,0:T(8,128)(2,1)}, u32[]{:S(2)}) copy-start(bf16[1024,512]{1,0:T(8,128)(2,1)} %param.26) | copy-start | bytes 3145732
  6.5 29.8 %copy-start.4 = (s32[196,1]{0,1:T(1,128)S(1)}, s32[196,1]{0,1:T(1,128)}, u32[]{:S(2)}) copy-start(s32[196,1]{0,1:T(1,128)} %param.19) | copy-start | bytes 2356
  6.5 30.1 %copy-start.8 = (s32[4]{0:T(128)S(1)}, s32[4]{0:T(128)}, u32[]{:S(2)}) copy-start(s32[4]{0:T(128)} %param.21) | copy-start | bytes 52
  6.5 94.7 %all-gather.5.cloned.1.call-start = ((), (), s32[]{:S(2)}) async-start(), calls=%async_computation.3 | async-start | bytes 4325376 | tf_op jit(solution)/shard_map/all_gather | solution.py:102
  7.3 182.0 %all-gather.7.cloned.1.call-start = ((), (), s32[]{:S(2)}) async-start(), calls=%async_computation.4 | async-start | bytes 4325376 | tf_op jit(solution)/shard_map/all_gather | solution.py:103
  12.6 17.1 %all-to-all-start.1 = ((bf16[16,1,24]{2,1,0:T(2,128)(2,1)}), bf16[16,1,24]{2,1,0:T(2,128)(2,1)S(1)}, u32[]{:S(2)}, u32[]{:S(2)}) async-start(bf16[16,1,24]{2,1,0:T(2,128)(2,1)} %all_to_all.16), calls=%async_computation.1 | async-start | bytes 16384 | tf_op jit(solution)/shard_map/all_to_all | solution.py:83
  29.7 64.0 %copy-start.5 = (f32[1024]{0:T(1024)S(1)}, f32[1024]{0:T(1024)}, u32[]{:S(2)}) copy-start(f32[1024]{0:T(1024)} %param.22) | copy-start | bytes 12292
  29.7 63.2 %all-to-all-start = ((bf16[16,24,1024]{2,1,0:T(8,128)(2,1)}), bf16[16,24,1024]{2,1,0:T(8,128)(2,1)S(1)}, u32[]{:S(2)}, u32[]{:S(2)}) async-start(bf16[16,24,1024]{2,1,0:T(8,128)(2,1)} %bitcast.22), calls=%async_computation | async-start | bytes 1572864 | tf_op jit(solution)/shard_map/all_to_all | solution.py:76
  196.3 16.0 %copy-start.7 = (s32[4,49]{1,0:T(4,128)S(1)}, s32[4,49]{1,0:T(4,128)}, u32[]{:S(2)}) copy-start(s32[4,49]{1,0:T(4,128)} %param.20) | copy-start | bytes 2356
  197.0 44.4 %copy-start.6 = (f32[1024]{0:T(1024)S(1)}, f32[1024]{0:T(1024)}, u32[]{:S(2)}) copy-start(f32[1024]{0:T(1024)} %param.25) | copy-start | bytes 12292
  198.3 44.3 %copy-start.1 = (bf16[512,512]{1,0:T(8,128)(2,1)S(1)}, bf16[512,512]{1,0:T(8,128)(2,1)}, u32[]{:S(2)}) copy-start(bf16[512,512]{1,0:T(8,128)(2,1)} %param.31) | copy-start | bytes 1572868
  198.3 44.3 %copy-start.2 = (f32[512]{0:T(512)S(1)}, f32[512]{0:T(512)}, u32[]{:S(2)}) copy-start(f32[512]{0:T(512)} %param.29) | copy-start | bytes 6148
  198.3 44.3 %copy-start.3 = (bf16[512]{0:T(512)(128)(2,1)S(1)}, bf16[512]{0:T(512)(128)(2,1)}, u32[]{:S(2)}) copy-start(bf16[512]{0:T(512)(128)(2,1)} %param.27) | copy-start | bytes 3076
  198.3 42.3 %all-to-all-start.2 = ((bf16[16,24,1024]{2,1,0:T(8,128)(2,1)}), bf16[16,24,1024]{2,1,0:T(8,128)(2,1)S(1)}, u32[]{:S(2)}, u32[]{:S(2)}) async-start(bf16[16,24,1024]{2,1,0:T(8,128)(2,1)} %copy.52), calls=%async_computation.2 | async-start | bytes 1572864 | tf_op jit(solution)/shard_map/all_to_all | solution.py:129
Sparse Core Ops, SparseCore 0:
  10.5 90.6 all-gather.4
  104.4 84.8 all-gather.6
where the time goes:
time: 294 us; the launch traced here: 293 us
  waiting for transfers between devices  101 us (34%)
  blocking collectives  83.8 us (29%)
  matrix products  50.2 us (17%)
  starting transfers between devices  25.2 us (9%)
  between operations  16.2 us (6%)
  local copies, waits for them, and re-layouts  9.71 us (3%)
  other arithmetic  6.8 us (2%)
    all_gather x1, waiting for transfers between devices, per_device(): piece_out = lax.all_gather(expert_out, 'dp', axis=1, tiled=True)  88 us
    unnamed x1, blocking collectives  55.7 us
    all_gather x1, blocking collectives, per_device(): lax.all_gather(visible, 'expert', axis=0, tiled=True)  28.1 us
    sub x4, matrix products, decode_image(): raised = jnp.exp(scores - highest)  12 us
    all_to_all x1, starting transfers between devices, per_device(): lax.all_to_all(outgoing, 'expert', split_axis=0, concat_axis=0, tiled=True)  10.9 us
    all_to_all x1, starting transfers between devices, per_device(): lax.all_to_all(send_weight.reshape(groups, exp_dev * capacity), 'expert',...  10.1 us
    dot_general x4, matrix products, decode_image(): jnp.einsum('ihqk,ikhc->iqhc', weights, value_rows, preferred_element_type...  9.58 us
    dot_general x4, matrix products, decode_image(): jnp.dot(dec_normed.reshape(GRID, DD), attention_in, preferred_element_typ...  7.77 us
  transfers between devices with their start and end apart: 5, of which 3 were waited for; matrix products, arithmetic and copies ran while one was open for 4% of the time, Pallas kernels for 0%

commit v1 on v0

--- a/solution.py
+++ b/solution.py
@@ -10,6 +10,24 @@
 GRID = 196
 VIS = 49
 EPSILON = 1e-06
+
+
+def collect(value, axis, dim):
+    ways, here, step = (lax.axis_size(axis), lax.axis_index(axis), value.shape[dim])
+    lengths = [n * ways if d == dim else n for d, n in enumerate(value.shape)]
+    full = lax.dynamic_update_slice_in_dim(
+        jnp.zeros(lengths, value.dtype), value, here * step, axis=dim
+    )
+    going_up = going_down = value
+    for far in range(1, ways // 2 + 1):
+        going_up = lax.ppermute(going_up, axis, [(d, (d + 1) % ways) for d in range(ways)])
+        full = lax.dynamic_update_slice_in_dim(full, going_up, (here - far) % ways * step, axis=dim)
+        if 2 * far < ways:
+            going_down = lax.ppermute(going_down, axis, [(d, (d - 1) % ways) for d in range(ways)])
+            full = lax.dynamic_update_slice_in_dim(
+                full, going_down, (here + far) % ways * step, axis=dim
+            )
+    return full
 
 
 def layer_norm(values, factor):
@@ -64,7 +82,7 @@
     token_expert = expert_ids[:, 0]
     all_ids, all_visible, all_owner = (
         lax.all_gather(token_expert, "expert", axis=0, tiled=True),
-        lax.all_gather(visible, "expert", axis=0, tiled=True),
+        collect(visible, "expert", 0),
         lax.all_gather(owner_map, "expert", axis=0, tiled=True),
     )
     placing = slot_table(token_expert, experts, capacity)

time: 294 us -> 297 us (1.010)
  blocking collectives: 83.8 us -> 45.9 us
  starting transfers between devices: 25.2 us -> 46.2 us
  waiting for transfers between devices: 101 us -> 118 us
    ppermute x0 -> x15, waiting for transfers between devices: none -> 36.6 us  [the longest x8 30.1 us: collect(): lax.ppermute(going_up, axis, [(d, (d + 1) % ways) for d in range(ways)])]
    all_gather x1 -> x0, blocking collectives: 28.1 us -> none  [per_device(): lax.all_gather(visible, 'expert', axis=0, tiled=True)]
    ppermute x0 -> x15, starting transfers between devices: none -> 20.1 us  [the longest x8 13.2 us: collect(): lax.ppermute(going_up, axis, [(d, (d + 1) % ways) for d in range(ways)])]
    all_gather x1, waiting for transfers between devices: 88 us -> 77.2 us  [per_device(): piece_out = lax.all_gather(expert_out, 'dp', axis=1, tiled=True)]
    unnamed x1, blocking collectives: 55.7 us -> 45.9 us
    all_gather x1, waiting for transfers between devices: 7.14 us -> 0.02 us  [per_device(): piece_in = lax.all_gather(expert_in, 'dp', axis=1, tiled=True)]
    all_to_all x1, starting transfers between devices: 4.19 us -> 9.02 us  [per_device(): lax.all_to_all(send_rows.reshape(groups, exp_dev * capacity, D), 'expert'...]
    all_to_all x1, waiting for transfers between devices: 4.69 us -> 0.01 us  [per_device(): lax.all_to_all(send_weight.reshape(groups, exp_dev * capacity), 'expert',...]
  transfers between devices with their start and end apart: 5 -> 20, of which waited for: 3 -> 13; matrix products, arithmetic and copies ran while one was open for 4% -> 7% of each run, Pallas kernels for 0% -> 0%
where the time goes in v1:
time: 297 us; the launch traced here: 295 us
  waiting for transfers between devices  118 us (40%)
  matrix products  50.2 us (17%)
  starting transfers between devices  46.2 us (16%)
  blocking collectives  45.9 us (15%)
  between operations  16.1 us (5%)
  local copies, waits for them, and re-layouts  11.1 us (4%)
  other arithmetic  6.71 us (2%)
    all_gather x1, waiting for transfers between devices, per_device(): piece_out = lax.all_gather(expert_out, 'dp', axis=1, tiled=True)  77.2 us
    unnamed x1, blocking collectives  45.9 us
    ppermute x8, waiting for transfers between devices, collect(): lax.ppermute(going_up, axis, [(d, (d + 1) % ways) for d in range(ways)])  30.1 us
    ppermute x8, starting transfers between devices, collect(): lax.ppermute(going_up, axis, [(d, (d + 1) % ways) for d in range(ways)])  13.2 us
    sub x4, matrix products, decode_image(): raised = jnp.exp(scores - highest)  12 us
    all_to_all x1, starting transfers between devices, per_device(): lax.all_to_all(outgoing, 'expert', split_axis=0, concat_axis=0, tiled=True)  10.9 us
    dot_general x4, matrix products, decode_image(): jnp.einsum('ihqk,ikhc->iqhc', weights, value_rows, preferred_element_type...  9.58 us
    all_to_all x1, starting transfers between devices, per_device(): lax.all_to_all(send_rows.reshape(groups, exp_dev * capacity, D), 'expert'...  9.02 us
  transfers between devices with their start and end apart: 20, of which 13 were waited for; matrix products, arithmetic and copies ran while one was open for 7% of the time, Pallas kernels for 0%

profile of v1, /device:TPU:1, one launch (start us, length us, event | category | flops | bytes accessed | tf_op | source)
XLA Modules:
  0.0 294.5 jit_solution(17449899454444884626)
XLA Ops:
  8.0 2.7 collective-permute-start
  10.7 4.2 %collective-permute-start.1 = (s32[4,49]{1,0:T(4,128)}, s32[4,49]{1,0:T(4,128)S(1)}, u32[]{:S(2)}, u32[]{:S(2)}) collective-permute-start(s32[4,49]{1,0:T(4,128)} %param.20), channel_id=1, source_target_pairs={{0,15},{1,0},{2,1},{3,2},{4,3},{5,4},{6,5},{7,6},{8,7},{9,8},{10,9... | collective-permute-start | bytes 2360 | tf_op jit(solution)/shard_map/ppermute | solution.py:26
  19.5 6.1 %all-to-all-start.1 = ((bf16[16,1,24]{2,1,0:T(2,128)(2,1)}), bf16[16,1,24]{2,1,0:T(2,128)(2,1)S(1)}, u32[]{:S(2)}, u32[]{:S(2)}) async-start(bf16[16,1,24]{2,1,0:T(2,128)(2,1)} %all_to_all.16), calls=%async_computation.1 | async-start | bytes 16384 | tf_op jit(solution)/shard_map/all_to_all | solution.py:101
  29.9 45.9 %all-reduce.4 = (s32[64]{0:T(128)S(1)}, s32[3136]{0:T(1024)S(1)}) all-reduce(s32[64]{0:T(128)S(1)} %dynamic-update-slice, s32[3136]{0:T(1024)S(1)} %dynamic-update-slice.1), channel_id=1, replica_groups=mesh['dp'=32,'expert'=16] {'expert'}, use_global_device_ids=true, to_apply=%add.2 | all-reduce | flops 3200 | bytes 25600
  76.0 2.4 convolution_convert_fusion.2
  79.0 9.0 %all-to-all-start = ((bf16[16,24,1024]{2,1,0:T(8,128)(2,1)}), bf16[16,24,1024]{2,1,0:T(8,128)(2,1)S(1)}, u32[]{:S(2)}, u32[]{:S(2)}) async-start(bf16[16,24,1024]{2,1,0:T(8,128)(2,1)} %bitcast.20), calls=%async_computation | async-start | bytes 1572864 | tf_op jit(solution)/shard_map/all_to_all | solution.py:94
  90.3 1.6 collective-permute-start.2
  92.1 11.2 %collective-permute-done.2 = s32[4,49]{1,0:T(4,128)S(1)} collective-permute-done((s32[4,49]{1,0:T(4,128)S(1)}, s32[4,49]{1,0:T(4,128)S(1)}, u32[]{:S(2)}, u32[]{:S(2)}) %collective-permute-start.2) | collective-permute-done | bytes 816 | tf_op jit(solution)/shard_map/ppermute | solution.py:23
  103.3 2.7 collective-permute-start.4
  107.7 3.0 %all-to-all-done = bf16[16,24,1024]{2,1,0:T(8,128)(2,1)S(1)} async-done(((bf16[16,24,1024]{2,1,0:T(8,128)(2,1)}), bf16[16,24,1024]{2,1,0:T(8,128)(2,1)S(1)}, u32[]{:S(2)}, u32[]{:S(2)}) %all-to-all-start) | async-done | bytes 786464 | tf_op jit(solution)/shard_map/all_to_all | solution.py:94
  111.9 77.2 %all-gather.6.cloned.1.call-done = bf16[1,2048,1024]{2,1,0:T(8,128)(2,1)} async-done(((bf16[1,64,1024]{2,1,0:T(8,128)(2,1)}), bf16[1,2048,1024]{2,1,0:T(8,128)(2,1)}) %all-gather.6.cloned.1.call-update) | async-done | bytes 4194320 | tf_op jit(solution)/shard_map/all_gather | solution.py:121
  189.1 7.1 %fusion.42 = bf16[384,1024]{1,0:T(8,128)(2,1)S(1)} fusion(bf16[1,2048,1024]{2,1,0:T(8,128)(2,1)} %all-gather.6.cloned.1.call-done, bf16[384,1024]{1,0:T(8,128)(2,1)S(1)} %bitcast.148, bf16[1,2048,1024]{2,1,0:T(8,128)(2,1)} %all-gather.4.cloned.1.call-done, bf16[16,24,1024]{2,1,0:T(8,128)(2,1)S(1)} %all-to-all-done, f32[384]{0:T(512)S(1)} %reshape.421), kind=kOutput, calls=%fused_computation.55 | convolution fusion | flops 3229876224 | bytes 10749440 | tf_op jit(solution)/shard_map/esf,efd->esd/dot_general | solution.py:125
  198.2 10.9 %all-to-all-start.2 = ((bf16[16,24,1024]{2,1,0:T(8,128)(2,1)}), bf16[16,24,1024]{2,1,0:T(8,128)(2,1)S(1)}, u32[]{:S(2)}, u32[]{:S(2)}) async-start(bf16[16,24,1024]{2,1,0:T(8,128)(2,1)} %copy.52), calls=%async_computation.2 | async-start | bytes 1572864 | tf_op jit(solution)/shard_map/all_to_all | solution.py:147
  210.8 13.6 %collective-permute-done.6 = s32[4,49]{1,0:T(4,128)S(1)} collective-permute-done((s32[4,49]{1,0:T(4,128)S(1)}, s32[4,49]{1,0:T(4,128)S(1)}, u32[]{:S(2)}, u32[]{:S(2)}) %collective-permute-start.6) | collective-permute-done | bytes 816 | tf_op jit(solution)/shard_map/ppermute | solution.py:23
  224.4 2.7 collective-permute-start.8
  227.1 1.6 collective-permute-done.7
  235.1 1.9 collective-permute-start.13
  238.1 3.7 %collective-permute-done.14 = s32[4,49]{1,0:T(4,128)S(1)} collective-permute-done((s32[4,49]{1,0:T(4,128)S(1)}, s32[4,49]{1,0:T(4,128)S(1)}, u32[]{:S(2)}, u32[]{:S(2)}) %collective-permute-start.14) | collective-permute-done | bytes 816 | tf_op jit(solution)/shard_map/ppermute | solution.py:23
  243.9 41.3 %while.10 = (s32[]{:T(128)}, bf16[4,1,196,512]{3,2,1,0:T(8,128)(2,1)}, s32[4,1,49]{2,1,0:T(1,128)S(1)}, bf16[4,1,49,512]{3,2,1,0:T(8,128)(2,1)}, bf16[512]{0:T(5...) while((s32[]{:T(128)}, ...), condition=%wide.region_17.18_spmd, body=%wide.region_11.17_spmd.sunk | while | flops 504361024 | bytes 12126609 | solution.py:191
  245.6 1.9 convolution_convert_fusion.6
  247.9 3.0 %fusion.93 = (f32[16,196]{1,0:T(8,128)S(1)}, f32[16,196,196]{1,2,0:T(8,128)}) fusion(bf16[1,196,3,16,32]{1,4,3,2,0:T(8,128)(2,1)S(1)} %bitcast.143), kind=kOutput, calls=%fused_computation.131.clone.1 | convolution fusion | flops 41182148 | bytes 2995456 | tf_op jit(solution)/shard_map/while/body/eval_jaxpr/sub | solution.py:181
  250.8 2.4 fusion.94
  256.0 1.9 convolution_convert_fusion.6
  258.2 3.0 %fusion.93 = (f32[16,196]{1,0:T(8,128)S(1)}, f32[16,196,196]{1,2,0:T(8,128)}) fusion(bf16[1,196,3,16,32]{1,4,3,2,0:T(8,128)(2,1)S(1)} %bitcast.143), kind=kOutput, calls=%fused_computation.131.clone.1 | convolution fusion | flops 41182148 | bytes 2995456 | tf_op jit(solution)/shard_map/while/body/eval_jaxpr/sub | solution.py:181
  261.2 2.4 fusion.94
  266.3 1.9 convolution_convert_fusion.6
  268.5 3.0 %fusion.93 = (f32[16,196]{1,0:T(8,128)S(1)}, f32[16,196,196]{1,2,0:T(8,128)}) fusion(bf16[1,196,3,16,32]{1,4,3,2,0:T(8,128)(2,1)S(1)} %bitcast.143), kind=kOutput, calls=%fused_computation.131.clone.1 | convolution fusion | flops 41182148 | bytes 2995456 | tf_op jit(solution)/shard_map/while/body/eval_jaxpr/sub | solution.py:181
  271.5 2.4 fusion.94
  276.6 1.9 convolution_convert_fusion.6
  278.8 3.0 %fusion.93 = (f32[16,196]{1,0:T(8,128)S(1)}, f32[16,196,196]{1,2,0:T(8,128)}) fusion(bf16[1,196,3,16,32]{1,4,3,2,0:T(8,128)(2,1)S(1)} %bitcast.143), kind=kOutput, calls=%fused_computation.131.clone.1 | convolution fusion | flops 41182148 | bytes 2995456 | tf_op jit(solution)/shard_map/while/body/eval_jaxpr/sub | solution.py:181
  281.8 2.4 fusion.94
  285.2 2.4 copy.67
  (144 shorter events, 38.9 us)
Async XLA Ops:
  6.5 236.1 %copy-start = (bf16[1024,512]{1,0:T(8,128)(2,1)S(1)}, bf16[1024,512]{1,0:T(8,128)(2,1)}, u32[]{:S(2)}) copy-start(bf16[1024,512]{1,0:T(8,128)(2,1)} %param.26) | copy-start | bytes 3145732
  6.5 83.6 %copy-start.6 = (s32[4,49]{1,0:T(4,128)S(1)}, s32[4,49]{1,0:T(4,128)}, u32[]{:S(2)}) copy-start(s32[4,49]{1,0:T(4,128)} %param.20) | copy-start | bytes 2356
  6.5 105.3 %all-gather.4.cloned.1.call-start = ((), (), s32[]{:S(2)}) async-start(), calls=%async_computation.3 | async-start | bytes 4325376 | tf_op jit(solution)/shard_map/all_gather | solution.py:120
  7.3 181.8 %all-gather.6.cloned.1.call-start = ((), (), s32[]{:S(2)}) async-start(), calls=%async_computation.4 | async-start | bytes 4325376 | tf_op jit(solution)/shard_map/all_gather | solution.py:121
  8.0 82.3 %collective-permute-start = (s32[4,49]{1,0:T(4,128)}, s32[4,49]{1,0:T(4,128)S(1)}, u32[]{:S(2)}, u32[]{:S(2)}) collective-permute-start(s32[4,49]{1,0:T(4,128)} %param.20), channel_id=1, source_target_pairs={{0,1},{1,2},{2,3},{3,4},{4,5},{5,6},{6,7},{7,8},{8,9},{9,10},{10,1... | collective-permute-start | bytes 2360 | tf_op jit(solution)/shard_map/ppermute | solution.py:23
  10.7 81.3 %collective-permute-start.1 = (s32[4,49]{1,0:T(4,128)}, s32[4,49]{1,0:T(4,128)S(1)}, u32[]{:S(2)}, u32[]{:S(2)}) collective-permute-start(s32[4,49]{1,0:T(4,128)} %param.20), channel_id=1, source_target_pairs={{0,15},{1,0},{2,1},{3,2},{4,3},{5,4},{6,5},{7,6},{8,7},{9,8},{10,9... | collective-permute-start | bytes 2360 | tf_op jit(solution)/shard_map/ppermute | solution.py:26
  19.5 59.5 %all-to-all-start.1 = ((bf16[16,1,24]{2,1,0:T(2,128)(2,1)}), bf16[16,1,24]{2,1,0:T(2,128)(2,1)S(1)}, u32[]{:S(2)}, u32[]{:S(2)}) async-start(bf16[16,1,24]{2,1,0:T(2,128)(2,1)} %all_to_all.16), calls=%async_computation.1 | async-start | bytes 16384 | tf_op jit(solution)/shard_map/all_to_all | solution.py:101
  79.0 32.6 %copy-start.4 = (f32[1024]{0:T(1024)S(1)}, f32[1024]{0:T(1024)}, u32[]{:S(2)}) copy-start(f32[1024]{0:T(1024)} %param.22) | copy-start | bytes 12292
  79.0 31.7 %all-to-all-start = ((bf16[16,24,1024]{2,1,0:T(8,128)(2,1)}), bf16[16,24,1024]{2,1,0:T(8,128)(2,1)S(1)}, u32[]{:S(2)}, u32[]{:S(2)}) async-start(bf16[16,24,1024]{2,1,0:T(8,128)(2,1)} %bitcast.20), calls=%async_computation | async-start | bytes 1572864 | tf_op jit(solution)/shard_map/all_to_all | solution.py:94
  90.3 13.0 %collective-permute-start.2 = (s32[4,49]{1,0:T(4,128)S(1)}, s32[4,49]{1,0:T(4,128)S(1)}, u32[]{:S(2)}, u32[]{:S(2)}) collective-permute-start(s32[4,49]{1,0:T(4,128)S(1)} %collective-permute-done), channel_id=1, source_target_pairs={{0,1},{1,2},{2,3},{3,4},{4,5},{5,6},{6,7},{7,8},{8,9},{9,10},{10,1... | collective-permute-start | bytes 2360 | tf_op jit(solution)/shard_map/ppermute | solution.py:23
  92.0 15.7 %collective-permute-start.3 = (s32[4,49]{1,0:T(4,128)S(1)}, s32[4,49]{1,0:T(4,128)S(1)}, u32[]{:S(2)}, u32[]{:S(2)}) collective-permute-start(s32[4,49]{1,0:T(4,128)S(1)} %collective-permute-done.1), channel_id=1, source_target_pairs={{0,15},{1,0},{2,1},{3,2},{4,3},{5,4},{6,5},{7,6},{8,7},{9,8},{10,9... | collective-permute-start | bytes 2360 | tf_op jit(solution)/shard_map/ppermute | solution.py:26
  103.3 105.8 %collective-permute-start.4 = (s32[4,49]{1,0:T(4,128)S(1)}, s32[4,49]{1,0:T(4,128)S(1)}, u32[]{:S(2)}, u32[]{:S(2)}) collective-permute-start(s32[4,49]{1,0:T(4,128)S(1)} %collective-permute-done.2), channel_id=1, source_target_pairs={{0,1},{1,2},{2,3},{3,4},{4,5},{5,6},{6,7},{7,8},{8,9},{9,10},{10,1... | collective-permute-start | bytes 2360 | tf_op jit(solution)/shard_map/ppermute | solution.py:23
  107.7 103.1 %collective-permute-start.5 = (s32[4,49]{1,0:T(4,128)S(1)}, s32[4,49]{1,0:T(4,128)S(1)}, u32[]{:S(2)}, u32[]{:S(2)}) collective-permute-start(s32[4,49]{1,0:T(4,128)S(1)} %collective-permute-done.3), channel_id=1, source_target_pairs={{0,15},{1,0},{2,1},{3,2},{4,3},{5,4},{6,5},{7,6},{8,7},{9,8},{10,9... | collective-permute-start | bytes 2360 | tf_op jit(solution)/shard_map/ppermute | solution.py:26
  196.8 45.8 %copy-start.5 = (f32[1024]{0:T(1024)S(1)}, f32[1024]{0:T(1024)}, u32[]{:S(2)}) copy-start(f32[1024]{0:T(1024)} %param.25) | copy-start | bytes 12292
  198.2 45.7 %copy-start.1 = (bf16[512,512]{1,0:T(8,128)(2,1)S(1)}, bf16[512,512]{1,0:T(8,128)(2,1)}, u32[]{:S(2)}) copy-start(bf16[512,512]{1,0:T(8,128)(2,1)} %param.31) | copy-start | bytes 1572868
  198.2 45.7 %copy-start.2 = (f32[512]{0:T(512)S(1)}, f32[512]{0:T(512)}, u32[]{:S(2)}) copy-start(f32[512]{0:T(512)} %param.29) | copy-start | bytes 6148
  198.2 45.7 %copy-start.3 = (bf16[512]{0:T(512)(128)(2,1)S(1)}, bf16[512]{0:T(512)(128)(2,1)}, u32[]{:S(2)}) copy-start(bf16[512]{0:T(512)(128)(2,1)} %param.27) | copy-start | bytes 3076
  198.2 43.7 %all-to-all-start.2 = ((bf16[16,24,1024]{2,1,0:T(8,128)(2,1)}), bf16[16,24,1024]{2,1,0:T(8,128)(2,1)S(1)}, u32[]{:S(2)}, u32[]{:S(2)}) async-start(bf16[16,24,1024]{2,1,0:T(8,128)(2,1)} %copy.52), calls=%async_computation.2 | async-start | bytes 1572864 | tf_op jit(solution)/shard_map/all_to_all | solution.py:147
  209.2 15.3 %collective-permute-start.6 = (s32[4,49]{1,0:T(4,128)S(1)}, s32[4,49]{1,0:T(4,128)S(1)}, u32[]{:S(2)}, u32[]{:S(2)}) collective-permute-start(s32[4,49]{1,0:T(4,128)S(1)} %collective-permute-done.4), channel_id=1, source_target_pairs={{0,1},{1,2},{2,3},{3,4},{4,5},{5,6},{6,7},{7,8},{8,9},{9,10},{10,1... | collective-permute-start | bytes 2360 | tf_op jit(solution)/shard_map/ppermute | solution.py:23
  210.8 18.0 %collective-permute-start.7 = (s32[4,49]{1,0:T(4,128)S(1)}, s32[4,49]{1,0:T(4,128)S(1)}, u32[]{:S(2)}, u32[]{:S(2)}) collective-permute-start(s32[4,49]{1,0:T(4,128)S(1)} %collective-permute-done.5), channel_id=1, source_target_pairs={{0,15},{1,0},{2,1},{3,2},{4,3},{5,4},{6,5},{7,6},{8,7},{9,8},{10,9... | collective-permute-start | bytes 2360 | tf_op jit(solution)/shard_map/ppermute | solution.py:26
  224.4 4.7 %collective-permute-start.8 = (s32[4,49]{1,0:T(4,128)S(1)}, s32[4,49]{1,0:T(4,128)S(1)}, u32[]{:S(2)}, u32[]{:S(2)}) collective-permute-start(s32[4,49]{1,0:T(4,128)S(1)} %collective-permute-done.6), channel_id=1, source_target_pairs={{0,1},{1,2},{2,3},{3,4},{4,5},{5,6},{6,7},{7,8},{8,9},{9,10},{10,1... | collective-permute-start | bytes 2360 | tf_op jit(solution)/shard_map/ppermute | solution.py:23
  228.8 3.3 %collective-permute-start.9 = (s32[4,49]{1,0:T(4,128)S(1)}, s32[4,49]{1,0:T(4,128)S(1)}, u32[]{:S(2)}, u32[]{:S(2)}) collective-permute-start(s32[4,49]{1,0:T(4,128)S(1)} %collective-permute-done.7), channel_id=1, source_target_pairs={{0,15},{1,0},{2,1},{3,2},{4,3},{5,4},{6,5},{7,6},{8,7},{9,8},{10,9... | collective-permute-start | bytes 2360 | tf_op jit(solution)/shard_map/ppermute | solution.py:26
  229.2 4.2 %collective-permute-start.10 = (s32[4,49]{1,0:T(4,128)S(1)}, s32[4,49]{1,0:T(4,128)S(1)}, u32[]{:S(2)}, u32[]{:S(2)}) collective-permute-start(s32[4,49]{1,0:T(4,128)S(1)} %collective-permute-done.8), channel_id=1, source_target_pairs={{0,1},{1,2},{2,3},{3,4},{4,5},{5,6},{6,7},{7,8},{8,9},{9,10},{10,1... | collective-permute-start | bytes 2360 | tf_op jit(solution)/shard_map/ppermute | solution.py:23
  232.1 3.0 %collective-permute-start.11 = (s32[4,49]{1,0:T(4,128)S(1)}, s32[4,49]{1,0:T(4,128)S(1)}, u32[]{:S(2)}, u32[]{:S(2)}) collective-permute-start(s32[4,49]{1,0:T(4,128)S(1)} %collective-permute-done.9), channel_id=1, source_target_pairs={{0,15},{1,0},{2,1},{3,2},{4,3},{5,4},{6,5},{7,6},{8,7},{9,8},{10,9... | collective-permute-start | bytes 2360 | tf_op jit(solution)/shard_map/ppermute | solution.py:26
  233.4 4.2 %collective-permute-start.12 = (s32[4,49]{1,0:T(4,128)S(1)}, s32[4,49]{1,0:T(4,128)S(1)}, u32[]{:S(2)}, u32[]{:S(2)}) collective-permute-start(s32[4,49]{1,0:T(4,128)S(1)} %collective-permute-done.10), channel_id=1, source_target_pairs={{0,1},{1,2},{2,3},{3,4},{4,5},{5,6},{6,7},{7,8},{8,9},{9,10},{10,1... | collective-permute-start | bytes 2360 | tf_op jit(solution)/shard_map/ppermute | solution.py:23
  235.1 3.0 %collective-permute-start.13 = (s32[4,49]{1,0:T(4,128)S(1)}, s32[4,49]{1,0:T(4,128)S(1)}, u32[]{:S(2)}, u32[]{:S(2)}) collective-permute-start(s32[4,49]{1,0:T(4,128)S(1)} %collective-permute-done.11), channel_id=1, source_target_pairs={{0,15},{1,0},{2,1},{3,2},{4,3},{5,4},{6,5},{7,6},{8,7},{9,8},{10,9... | collective-permute-start | bytes 2360 | tf_op jit(solution)/shard_map/ppermute | solution.py:26
  237.6 4.2 %collective-permute-start.14 = (s32[4,49]{1,0:T(4,128)S(1)}, s32[4,49]{1,0:T(4,128)S(1)}, u32[]{:S(2)}, u32[]{:S(2)}) collective-permute-start(s32[4,49]{1,0:T(4,128)S(1)} %collective-permute-done.12), channel_id=1, source_target_pairs={{0,1},{1,2},{2,3},{3,4},{4,5},{5,6},{6,7},{7,8},{8,9},{9,10},{10,1... | collective-permute-start | bytes 2360 | tf_op jit(solution)/shard_map/ppermute | solution.py:23
Sparse Core Ops, SparseCore 0:
  10.5 90.5 all-gather.3
  104.3 84.7 all-gather.5
